TPU v7x, 256 devices: a whole 4x4x8 slice. The times are simulated.
256 devices in a mesh: dp: 2 (over y_hi), pipe: 16 (over y_lo, x, core), seq: 8 (over z).
Axes of the slice: x: 4, y: 4 (y_hi: 2, y_lo: 2; y = y_hi * 2 + y_lo), z: 8, core: 2. Of those that a mesh axis runs over, the one named last changes fastest.
Arguments:
- enc_out: bfloat16 [2, 512, 4096], P('dp', None, 'seq'), may hold values from -60 to 60
- w_key: bfloat16 [16, 4096, 2048], P('pipe', None, 'seq'), may hold values from -0.125 to 0.125
- w_value: bfloat16 [16, 4096, 2048], P('pipe', None, 'seq'), may hold values from -0.125 to 0.125
- query: bfloat16 [16, 2, 512, 2048], P('pipe', 'dp', None, 'seq'), may hold values from -256 to 256
- key_cache: bfloat16 [16, 2, 512, 2048], P('pipe', 'dp', None, 'seq'), may hold values from -6 to 6
- value_cache: bfloat16 [16, 2, 512, 2048], P('pipe', 'dp', None, 'seq'), may hold values from -6 to 6
- grad_attn: bfloat16 [16, 2, 512, 2048], P('pipe', 'dp', None, 'seq'), may hold values from -200 to 200
- dec_segments: int32 [2, 512], P('dp'), may hold values from 0 to 3, as said below
- enc_segments: int32 [2, 512], P('dp'), may hold values from 0 to 3, as said below
Outputs:
- grad_query: bfloat16 [16, 2, 512, 2048], P('pipe', 'dp', None, 'seq')
- grad_enc: float32 [2, 512, 4096], P('dp', 'seq', 'pipe')
- grad_wkey: float32 [16, 4096, 2048], P('pipe', 'dp', 'seq')
- grad_wvalue: float32 [16, 4096, 2048], P('pipe', 'dp', 'seq')
Inputs may be any that keep to these rules, and one draw needn't show every extreme that they name: `dec_segments`: never falling along a sequence; every number from 0 to 3 occurs; a segment holds 1 to 256 tokens, and one holds exactly 256. `enc_segments`: never falling along a sequence; every number from 0 to 3 occurs; a segment holds 1 to 256 tokens, and one holds exactly 256.
All inputs are finite; a program needn't handle non-finite values.
Results may differ from a plain program's by a relative error of at most 0.006.
Values may be sent and summed in bfloat16 or wider, within the bound.
No kernel may reach another device: no remote copies, remote signals or barrier semaphores. Data moves between devices by JAX's collectives and lax.ppermute only.
A program may use at most 128 MiB of HBM per device.

v0:
```python
import math
import jax
import jax.numpy as jnp
from jax import lax
from jax.sharding import PartitionSpec as P

D = 4096
H = 8
HD = 256


def head_backward(query_heads, key_heads, value_heads, grad_heads, dec_ids, enc_ids):
    length = query_heads.shape[0]
    block_rows = 512
    block_count = length // block_rows
    inverse_root = 1.0 / math.sqrt(query_heads.shape[2])

    def block_step(partial_value, block_index):
        acc_key, acc_value = partial_value
        same_segment = dec_ids[:, None] == enc_ids[None, :]
        scores = (
            jnp.einsum("qhd,khd->hqk", query_heads, key_heads, preferred_element_type=jnp.float32)
            * inverse_root
        )
        scores = jnp.where(same_segment[None], scores, -jnp.inf)
        row_max = jnp.max(scores, axis=2, keepdims=True)
        exp_scores = jnp.exp(scores - row_max)
        probs_full = exp_scores / jnp.sum(exp_scores, axis=2, keepdims=True)
        dprobs = jnp.einsum(
            "qhd,khd->hqk", grad_heads, value_heads, preferred_element_type=jnp.float32
        )
        row_delta = jnp.sum(probs_full * dprobs, axis=2, keepdims=True)
        dscores = (probs_full * (dprobs - row_delta) * inverse_root).astype(jnp.bfloat16)
        probs_low = probs_full.astype(jnp.bfloat16)
        query_grad = jnp.einsum(
            "hqk,khd->qhd", dscores, key_heads, preferred_element_type=jnp.float32
        ).astype(jnp.bfloat16)
        acc_key = acc_key + jnp.einsum(
            "hqk,qhd->khd", dscores, query_heads, preferred_element_type=jnp.float32
        )
        acc_value = acc_value + jnp.einsum(
            "hqk,qhd->khd", probs_low, grad_heads, preferred_element_type=jnp.float32
        )
        return ((acc_key, acc_value), query_grad)

    zeros_init = jnp.zeros(key_heads.shape, jnp.float32)
    (acc_key, acc_value), query_blocks = lax.scan(
        block_step, (zeros_init, zeros_init), jnp.arange(block_count, dtype=jnp.int32)
    )
    query_grad = query_blocks.reshape(query_heads.shape)
    return (query_grad, acc_key.astype(jnp.bfloat16), acc_value.astype(jnp.bfloat16))


def shards(
    enc_out, w_key, w_value, query, key_cache, value_cache, grad_attn, dec_segments, enc_segments
):
    length = query.shape[2]
    columns = query.shape[3]
    local_heads = columns // HD
    head_shape = (length, local_heads, HD)
    query_grad, grad_keys, grad_values = head_backward(
        query[0, 0].reshape(head_shape),
        key_cache[0, 0].reshape(head_shape),
        value_cache[0, 0].reshape(head_shape),
        grad_attn[0, 0].reshape(head_shape),
        dec_segments[0],
        enc_segments[0],
    )
    grad_query = query_grad.reshape(1, 1, length, columns)
    keys_flat = grad_keys.reshape(length, columns)
    values_flat = grad_values.reshape(length, columns)
    section_wkey = w_key[0]
    section_wvalue = w_value[0]
    column_contract = (((1,), (1,)), ((), ()))
    by_section = lax.psum_scatter(
        lax.dot_general(
            section_wkey, keys_flat, column_contract, preferred_element_type=jnp.float32
        )
        + lax.dot_general(
            section_wvalue, values_flat, column_contract, preferred_element_type=jnp.float32
        ),
        "pipe",
        scatter_dimension=0,
        tiled=True,
    )
    by_head = lax.psum_scatter(by_section, "seq", scatter_dimension=1, tiled=True)
    grad_enc = jnp.transpose(by_head)[None]
    token_contract = (((0,), (0,)), ((), ()))
    grad_both = jnp.concatenate([keys_flat, values_flat], axis=1)
    both_sums = lax.dot_general(
        lax.all_gather(enc_out, "seq", axis=2, tiled=True)[0],
        grad_both,
        token_contract,
        preferred_element_type=jnp.float32,
    )
    sum_key = both_sums[:, :columns]
    sum_value = both_sums[:, columns:]
    share_key, share_value = (
        lax.psum_scatter(sum_key, "dp", scatter_dimension=0, tiled=True),
        lax.psum_scatter(sum_value, "dp", scatter_dimension=0, tiled=True),
    )
    square_key, square_value = lax.psum(
        (jnp.sum(share_key * share_key), jnp.sum(share_value * share_value)), ("dp", "seq")
    )
    entries = D * H * HD
    grad_wkey = (share_key / jnp.sqrt(square_key / entries + 1e-06))[None]
    grad_wvalue = (share_value / jnp.sqrt(square_value / entries + 1e-06))[None]
    return (grad_query, grad_enc, grad_wkey, grad_wvalue)


def solution(mesh):
    in_specs = (
        P("dp", None, "seq"),
        P("pipe", None, "seq"),
        P("pipe", None, "seq"),
        P("pipe", "dp", None, "seq"),
        P("pipe", "dp", None, "seq"),
        P("pipe", "dp", None, "seq"),
        P("pipe", "dp", None, "seq"),
        P("dp", None),
        P("dp", None),
    )
    out_specs = (
        P("pipe", "dp", None, "seq"),
        P("dp", "seq", "pipe"),
        P("pipe", "dp", "seq"),
        P("pipe", "dp", "seq"),
    )
    return jax.shard_map(shards, mesh=mesh, in_specs=in_specs, out_specs=out_specs, check_vma=False)
```

profile of v0, /device:TPU:4, one launch (start us, length us, event | category | flops | bytes accessed | tf_op | source)
XLA Modules:
  0.0 323.7 jit_solution(271857215477745825)
XLA Ops:
  7.2 0.0 all-gather.2.cloned.1.call-start
  7.2 0.7 all-gather.2.cloned.1.call-update
  7.9 0.0 reduce-scatter.9.cloned.1.call-start
  8.0 1.4 fusion.23
  9.4 0.2 fusion.7
  9.6 0.4 multiply_reduce_fusion.2
  10.0 0.3 multiply_convert_fusion
  10.2 0.6 copy-done.2
  10.9 0.3 convolution_convert_fusion.1
  11.2 0.4 convolution_convert_fusion
  11.7 55.8 %all-gather.2.cloned.1.call-done = bf16[1,512,4096]{2,1,0:T(8,128)(2,1)} async-done(((bf16[1,512,512]{2,1,0:T(8,128)(2,1)}), bf16[1,512,4096]{2,1,0:T(8,128)(2,1)}) %all-gather.2.cloned.1.call-update) | async-done | bytes 4194320 | tf_op jit(solution)/shard_map/all_gather | solution.py:91
  67.5 4.5 %convolution_bitcast_fusion = f32[4096,512]{0,1:T(8,128)S(1)} fusion(bf16[1,512,4096]{2,1,0:T(8,128)(2,1)} %all-gather.2.cloned.1.call-done, bf16[512,256]{0,1:T(8,128)(2,1)S(1)} %convolution_convert_fusion, bf16[512,256]{0,1:T(8,128)(2,1)S(1)} %convolution_convert_fusion.1), kind=kOutput, calls=%fused_computation.1 | convolution fusion | flops 2148532224 | bytes 13107200 | tf_op jit(solution)/shard_map/dot_general | solution.py:90
  72.1 3.8 %fusion.22 = (f32[4096,256]{0,1:T(8,128)}, f32[4096,256]{0,1:T(8,128)}) fusion(f32[4096,512]{0,1:T(8,128)S(1)} %convolution_bitcast_fusion), kind=kLoop, calls=%fused_computation.34 | loop fusion | bytes 16777216 | tf_op jit(solution)/shard_map/slice | solution.py:97
  75.8 0.0 reduce-scatter.11.cloned.1.call-start
  75.9 0.7 reduce-scatter.11.cloned.1.call-update
  76.6 0.0 reduce-scatter.5.cloned.1.call-start
  76.6 1.3 fusion.2
  77.9 0.3 copy-done.1
  78.2 4.5 %add_bitcast_fusion = f32[4096,512]{0,1:T(8,128)} fusion(f32[512,4096]{1,0:T(8,128)S(1)} %fusion.2, bf16[512,256]{0,1:T(8,128)(2,1)S(1)} %convolution_convert_fusion, bf16[1,4096,256]{2,1,0:T(8,128)(2,1)S(1)} %copy-done.1), kind=kOutput, calls=%fused_computation | convolution fusion | flops 1075838976 | bytes 19136512 | tf_op jit(solution)/shard_map/dot_general | solution.py:79
  82.8 0.0 reduce-scatter.7.cloned.1.call-start
  82.8 52.7 %reduce-scatter.9.cloned.1.call-done = f32[2048,256]{0,1:T(8,128)} async-done(((f32[4096,256]{0,1:T(8,128)}), f32[2048,256]{0,1:T(8,128)}) %reduce-scatter.9.cloned.1.call-update) | async-done | bytes 2097168 | tf_op jit(solution)/shard_map/reduce_scatter | solution.py:99
  135.6 2.7 multiply_reduce_fusion.1
  138.3 60.3 %reduce-scatter.11.cloned.1.call-done = f32[2048,256]{0,1:T(8,128)} async-done(((f32[4096,256]{0,1:T(8,128)}), f32[2048,256]{0,1:T(8,128)}) %reduce-scatter.11.cloned.1.call-update) | async-done | bytes 2097168 | tf_op jit(solution)/shard_map/reduce_scatter | solution.py:100
  198.6 2.7 multiply_reduce_fusion
  201.3 1.1 fusion.5
  202.4 40.5 %all-reduce = (f32[]{:T(128)}, f32[]{:T(128)}) all-reduce(f32[]{:T(128)} %multiply_reduce_fusion.1, f32[]{:T(128)} %multiply_reduce_fusion), channel_id=1, replica_groups=mesh['dp'=2,'pipe'=16,'seq'=8] {'dp','seq'}, use_global_device_ids=true, to_apply=%region_7.8 | all-reduce | flops 2 | bytes 16 | tf_op jit(solution)/shard_map/psum | solution.py:102
  243.6 26.8 %reduce-scatter.5.cloned.1.call-done = f32[256,512]{0,1:T(8,128)} async-done(((f32[4096,512]{0,1:T(8,128)}), f32[256,512]{0,1:T(8,128)}) %reduce-scatter.5.cloned.1.call-update) | async-done | bytes 524304 | tf_op jit(solution)/shard_map/reduce_scatter | solution.py:75
  270.4 3.2 divide_bitcast_fusion.1
  273.6 2.9 copy.13
  277.1 3.2 divide_bitcast_fusion
  280.4 2.9 copy.14
  283.2 33.9 %reduce-scatter.7.cloned.1.call-done = f32[256,64]{0,1:T(8,128)} async-done(((f32[256,512]{0,1:T(8,128)}), f32[256,64]{0,1:T(8,128)}) %reduce-scatter.7.cloned.1.call-update) | async-done | bytes 65552 | tf_op jit(solution)/shard_map/reduce_scatter | solution.py:86
  (13 shorter events, 0.1 us)
Async XLA Ops:
  7.2 69.5 %copy-start = (bf16[1,4096,256]{2,1,0:T(8,128)(2,1)S(1)}, bf16[1,4096,256]{2,1,0:T(8,128)(2,1)}, u32[]{:S(2)}) copy-start(bf16[1,4096,256]{2,1,0:T(8,128)(2,1)} %param.10) | copy-start | bytes 6291460
  7.2 2.4 copy-start.3
  7.2 2.4 copy-start.4
  7.2 60.3 %all-gather.2.cloned.1.call-start = ((), (), s32[]{:S(2)}) async-start(), calls=%async_computation.6 | async-start | bytes 4718592 | tf_op jit(solution)/shard_map/all_gather | solution.py:91
  7.9 127.6 %reduce-scatter.9.cloned.1.call-start = ((), (), s32[]{:S(2)}) async-start(), calls=%async_computation.7 | async-start | bytes 6291456 | tf_op jit(solution)/shard_map/reduce_scatter | solution.py:99
  9.9 1.0 copy-start.2
  75.8 122.7 %reduce-scatter.11.cloned.1.call-start = ((), (), s32[]{:S(2)}) async-start(), calls=%async_computation.8 | async-start | bytes 6291456 | tf_op jit(solution)/shard_map/reduce_scatter | solution.py:100
  76.6 193.8 %reduce-scatter.5.cloned.1.call-start = ((), (), s32[]{:S(2)}) async-start(), calls=%async_computation.4 | async-start | bytes 8912896 | tf_op jit(solution)/shard_map/reduce_scatter | solution.py:75
  76.6 1.6 copy-start.1
  82.8 118.5 %copy-start.5 = (bf16[1,1,512,256]{3,2,1,0:T(8,128)(2,1)S(1)}, bf16[1,1,512,256]{3,2,1,0:T(8,128)(2,1)}, u32[]{:S(2)}) copy-start(bf16[1,1,512,256]{3,2,1,0:T(8,128)(2,1)} %param.13) | copy-start | bytes 786436
  82.8 234.4 %reduce-scatter.7.cloned.1.call-start = ((), (), s32[]{:S(2)}) async-start(), calls=%async_computation.5 | async-start | bytes 589824 | tf_op jit(solution)/shard_map/reduce_scatter | solution.py:86
Sparse Core Ops, SparseCore 0:
  9.8 57.6 all-gather.1
  76.0 59.5 reduce-scatter.8
  138.1 60.3 reduce-scatter.10
  201.0 69.4 reduce-scatter.4
  273.3 43.7 reduce-scatter.6
where the time goes:
time: 324 us
  waiting for transfers between devices  231 us (71%)
  blocking collectives  40.5 us (12%)
  between operations  15.2 us (5%)
  matrix products  13.9 us (4%)
  other arithmetic  12.4 us (4%)
  local copies, waits for them, and re-layouts  10.5 us (3%)
    reduce_scatter x1, waiting for transfers between devices, shards(): lax.psum_scatter(sum_value, 'dp', scatter_dimension=0, tiled=True)  60.3 us
    all_gather x1, waiting for transfers between devices, shards(): lax.all_gather(enc_out, 'seq', axis=2, tiled=True)[0]  55.8 us
    reduce_scatter x1, waiting for transfers between devices, shards(): lax.psum_scatter(sum_key, 'dp', scatter_dimension=0, tiled=True)  52.7 us
    psum x1, blocking collectives, shards(): lax.psum((jnp.sum(share_key * share_key), jnp.sum(share_value * share_val...  40.5 us
    reduce_scatter x1, waiting for transfers between devices, shards(): lax.psum_scatter(by_section, 'seq', scatter_dimension=1, tiled=True)  33.9 us
    reduce_scatter x1, waiting for transfers between devices, shards(): lax.psum_scatter(lax.dot_general(section_wkey, keys_flat, column_contract...  26.8 us
    unnamed x14, local copies, waits for them, and re-layouts  6.71 us
  transfers between devices with their start and end apart: 5, of which 5 were waited for; matrix products, arithmetic and copies ran while one was open for 9% of the time, Pallas kernels for 0%

commit v1 on v0

--- a/solution.py
+++ b/solution.py
@@ -88,7 +88,9 @@
     token_contract = (((0,), (0,)), ((), ()))
     grad_both = jnp.concatenate([keys_flat, values_flat], axis=1)
     both_sums = lax.dot_general(
-        lax.all_gather(enc_out, "seq", axis=2, tiled=True)[0],
+        jnp.concatenate(
+            lax.all_to_all(jnp.stack([enc_out] * lax.axis_size("seq")), "seq", 0, 0), axis=2
+        )[0],
         grad_both,
         token_contract,
         preferred_element_type=jnp.float32,

time: 324 us -> 371 us (1.15)
  waiting for transfers between devices: 231 us -> 266 us
  starting transfers between devices: 0.2 us -> 8.77 us
    all_to_all x0 -> x1, waiting for transfers between devices: none -> 93.9 us  [shards(): lax.all_to_all(jnp.stack([enc_out] * lax.axis_size('seq')), 'seq', 0, 0)]
    all_gather x1 -> x0, waiting for transfers between devices: 55.8 us -> none  [shards(): lax.all_gather(enc_out, 'seq', axis=2, tiled=True)[0]]
    all_to_all x0 -> x1, starting transfers between devices: none -> 8.61 us  [shards(): lax.all_to_all(jnp.stack([enc_out] * lax.axis_size('seq')), 'seq', 0, 0)]
    another operation x0 -> x2, local copies, waits for them, and re-layouts: none -> 3.73 us  [the longest x1 2.33 us: shards(): jnp.stack([enc_out] * lax.axis_size('seq'))]
  transfers between devices with their start and end apart: 5 -> 5, of which waited for: 5 -> 5; matrix products, arithmetic and copies ran while one was open for 9% -> 7% of each run, Pallas kernels for 0% -> 0%
where the time goes in v1:
time: 371 us; the launch traced here: 370 us
  waiting for transfers between devices  266 us (72%)
  blocking collectives  40.5 us (11%)
  between operations  15.2 us (4%)
  local copies, waits for them, and re-layouts  13.9 us (4%)
  matrix products  12.9 us (3%)
  other arithmetic  12.4 us (3%)
  starting transfers between devices  8.77 us (2%)
    all_to_all x1, waiting for transfers between devices, shards(): lax.all_to_all(jnp.stack([enc_out] * lax.axis_size('seq')), 'seq', 0, 0)  93.9 us
    reduce_scatter x1, waiting for transfers between devices, shards(): lax.psum_scatter(sum_value, 'dp', scatter_dimension=0, tiled=True)  60.3 us
    reduce_scatter x1, waiting for transfers between devices, shards(): lax.psum_scatter(sum_key, 'dp', scatter_dimension=0, tiled=True)  50.4 us
    psum x1, blocking collectives, shards(): lax.psum((jnp.sum(share_key * share_key), jnp.sum(share_value * share_val...  40.5 us
    reduce_scatter x1, waiting for transfers between devices, shards(): lax.psum_scatter(by_section, 'seq', scatter_dimension=1, tiled=True)  33.7 us
    reduce_scatter x1, waiting for transfers between devices, shards(): lax.psum_scatter(lax.dot_general(section_wkey, keys_flat, column_contract...  27.2 us
    all_to_all x1, starting transfers between devices, shards(): lax.all_to_all(jnp.stack([enc_out] * lax.axis_size('seq')), 'seq', 0, 0)  8.61 us
  transfers between devices with their start and end apart: 5, of which 5 were waited for; matrix products, arithmetic and copies ran while one was open for 7% of the time, Pallas kernels for 0%

profile of v1, /device:TPU:4, one launch (start us, length us, event | category | flops | bytes accessed | tf_op | source)
XLA Modules:
  0.0 370.0 jit_solution(9147246999617725597)
XLA Ops:
  7.2 1.4 copy.18
  8.6 2.3 stack.2
  10.9 8.6 %all-to-all-start = ((bf16[8,1,512,512]{2,3,1,0:T(8,128)(2,1)}), bf16[8,1,512,512]{2,3,1,0:T(8,128)(2,1)}, u32[]{:S(2)}, u32[]{:S(2)}) async-start(bf16[8,1,512,512]{2,3,1,0:T(8,128)(2,1)} %stack.2), calls=%async_computation.2 | async-start | bytes 8388608 | tf_op jit(solution)/shard_map/all_to_all | solution.py:92
  19.6 0.0 reduce-scatter.9.cloned.1.call-start
  19.6 0.3 fusion.22
  20.0 0.2 fusion.6
  20.2 0.3 copy-done.3
  20.5 0.1 copy-done.4
  20.6 0.4 multiply_reduce_fusion.2
  20.9 0.3 multiply_convert_fusion
  21.2 0.3 convolution_convert_fusion.1
  21.6 0.4 convolution_convert_fusion
  22.0 93.9 %all-to-all-done = bf16[8,1,512,512]{2,3,1,0:T(8,128)(2,1)} async-done(((bf16[8,1,512,512]{2,3,1,0:T(8,128)(2,1)}), bf16[8,1,512,512]{2,3,1,0:T(8,128)(2,1)}, u32[]{:S(2)}, u32[]{:S(2)}) %all-to-all-start) | async-done | bytes 4194336 | tf_op jit(solution)/shard_map/all_to_all | solution.py:92
  115.9 4.6 %convolution_bitcast_fusion = f32[4096,512]{0,1:T(8,128)S(1)} fusion(bf16[512,4096]{0,1:T(8,128)(2,1)} %bitcast.18, bf16[512,256]{0,1:T(8,128)(2,1)S(1)} %convolution_convert_fusion, bf16[512,256]{0,1:T(8,128)(2,1)S(1)} %convolution_convert_fusion.1), kind=kOutput, calls=%fused_computation.1 | convolution fusion | flops 2148532224 | bytes 13107200 | tf_op jit(solution)/shard_map/dot_general | solution.py:90
  120.5 3.8 %fusion.21 = (f32[4096,256]{0,1:T(8,128)}, f32[4096,256]{0,1:T(8,128)}) fusion(f32[4096,512]{0,1:T(8,128)S(1)} %convolution_bitcast_fusion), kind=kLoop, calls=%fused_computation.33 | loop fusion | bytes 16777216 | tf_op jit(solution)/shard_map/slice | solution.py:99
  124.3 0.7 reduce-scatter.11.cloned.1.call-update
  125.1 1.3 fusion.1
  126.4 0.3 copy-done.1
  126.7 4.5 %add_bitcast_fusion = f32[4096,512]{0,1:T(8,128)} fusion(f32[512,4096]{1,0:T(8,128)S(1)} %fusion.1, bf16[512,256]{0,1:T(8,128)(2,1)S(1)} %convolution_convert_fusion, bf16[1,4096,256]{2,1,0:T(8,128)(2,1)S(1)} %copy-done.1), kind=kOutput, calls=%fused_computation | convolution fusion | flops 1075838976 | bytes 19136512 | tf_op jit(solution)/shard_map/dot_general | solution.py:79
  131.2 0.0 reduce-scatter.7.cloned.1.call-start
  131.3 50.4 %reduce-scatter.9.cloned.1.call-done = f32[2048,256]{0,1:T(8,128)} async-done(((f32[4096,256]{0,1:T(8,128)}), f32[2048,256]{0,1:T(8,128)}) %reduce-scatter.9.cloned.1.call-update) | async-done | bytes 2097168 | tf_op jit(solution)/shard_map/reduce_scatter | solution.py:101
  181.7 2.7 multiply_reduce_fusion.1
  184.4 60.3 %reduce-scatter.11.cloned.1.call-done = f32[2048,256]{0,1:T(8,128)} async-done(((f32[4096,256]{0,1:T(8,128)}), f32[2048,256]{0,1:T(8,128)}) %reduce-scatter.11.cloned.1.call-update) | async-done | bytes 2097168 | tf_op jit(solution)/shard_map/reduce_scatter | solution.py:102
  244.7 2.7 multiply_reduce_fusion
  247.5 1.1 fusion.4
  248.5 40.5 %all-reduce = (f32[]{:T(128)}, f32[]{:T(128)}) all-reduce(f32[]{:T(128)} %multiply_reduce_fusion.1, f32[]{:T(128)} %multiply_reduce_fusion), channel_id=1, replica_groups=mesh['dp'=2,'pipe'=16,'seq'=8] {'dp','seq'}, use_global_device_ids=true, to_apply=%region_7.8 | all-reduce | flops 2 | bytes 16 | tf_op jit(solution)/shard_map/psum | solution.py:104
  289.7 27.2 %reduce-scatter.5.cloned.1.call-done = f32[256,512]{0,1:T(8,128)} async-done(((f32[4096,512]{0,1:T(8,128)}), f32[256,512]{0,1:T(8,128)}) %reduce-scatter.5.cloned.1.call-update) | async-done | bytes 524304 | tf_op jit(solution)/shard_map/reduce_scatter | solution.py:75
  316.9 3.2 divide_bitcast_fusion.1
  320.1 2.9 copy.20
  323.6 3.2 divide_bitcast_fusion
  326.8 2.9 copy.21
  329.7 33.7 %reduce-scatter.7.cloned.1.call-done = f32[256,64]{0,1:T(8,128)} async-done(((f32[256,512]{0,1:T(8,128)}), f32[256,64]{0,1:T(8,128)}) %reduce-scatter.7.cloned.1.call-update) | async-done | bytes 65552 | tf_op jit(solution)/shard_map/reduce_scatter | solution.py:86
  (20 shorter events, 0.2 us)
Async XLA Ops:
  7.2 117.9 %copy-start = (bf16[1,4096,256]{2,1,0:T(8,128)(2,1)S(1)}, bf16[1,4096,256]{2,1,0:T(8,128)(2,1)}, u32[]{:S(2)}) copy-start(bf16[1,4096,256]{2,1,0:T(8,128)(2,1)} %param.10) | copy-start | bytes 6291460
  10.9 8.7 %copy-start.2 = (bf16[1,1,512,256]{3,2,1,0:T(8,128)(2,1)S(1)}, bf16[1,1,512,256]{3,2,1,0:T(8,128)(2,1)}, u32[]{:S(2)}) copy-start(bf16[1,1,512,256]{3,2,1,0:T(8,128)(2,1)} %param.12) | copy-start | bytes 786436
  10.9 8.7 %copy-start.5 = (bf16[1,1,512,256]{3,2,1,0:T(8,128)(2,1)S(1)}, bf16[1,1,512,256]{3,2,1,0:T(8,128)(2,1)}, u32[]{:S(2)}) copy-start(bf16[1,1,512,256]{3,2,1,0:T(8,128)(2,1)} %param.13) | copy-start | bytes 786436
  10.9 8.7 %copy-start.7 = (s32[1,512]{1,0:T(1,128)S(1)}, s32[1,512]{1,0:T(1,128)}, u32[]{:S(2)}) copy-start(s32[1,512]{1,0:T(1,128)} %param.17) | copy-start | bytes 6148
  10.9 8.7 %copy-start.8 = (s32[1,512]{1,0:T(1,128)S(1)}, s32[1,512]{1,0:T(1,128)}, u32[]{:S(2)}) copy-start(s32[1,512]{1,0:T(1,128)} %param.16) | copy-start | bytes 6148
  10.9 105.0 %all-to-all-start = ((bf16[8,1,512,512]{2,3,1,0:T(8,128)(2,1)}), bf16[8,1,512,512]{2,3,1,0:T(8,128)(2,1)}, u32[]{:S(2)}, u32[]{:S(2)}) async-start(bf16[8,1,512,512]{2,3,1,0:T(8,128)(2,1)} %stack.2), calls=%async_computation.2 | async-start | bytes 8388608 | tf_op jit(solution)/shard_map/all_to_all | solution.py:92
  19.5 0.9 copy-start.3
  19.5 1.0 copy-start.4
  19.6 162.2 %reduce-scatter.9.cloned.1.call-start = ((), (), s32[]{:S(2)}) async-start(), calls=%async_computation.7 | async-start | bytes 6291456 | tf_op jit(solution)/shard_map/reduce_scatter | solution.py:101
  124.3 120.5 %reduce-scatter.11.cloned.1.call-start = ((), (), s32[]{:S(2)}) async-start(), calls=%async_computation.8 | async-start | bytes 6291456 | tf_op jit(solution)/shard_map/reduce_scatter | solution.py:102
  125.0 191.9 %reduce-scatter.5.cloned.1.call-start = ((), (), s32[]{:S(2)}) async-start(), calls=%async_computation.5 | async-start | bytes 8912896 | tf_op jit(solution)/shard_map/reduce_scatter | solution.py:75
  125.1 1.6 copy-start.1
  131.2 116.2 %copy-start.6 = (bf16[1,1,512,256]{3,2,1,0:T(8,128)(2,1)S(1)}, bf16[1,1,512,256]{3,2,1,0:T(8,128)(2,1)}, u32[]{:S(2)}) copy-start(bf16[1,1,512,256]{3,2,1,0:T(8,128)(2,1)} %param.13) | copy-start | bytes 786436
  131.2 232.2 %reduce-scatter.7.cloned.1.call-start = ((), (), s32[]{:S(2)}) async-start(), calls=%async_computation.6 | async-start | bytes 589824 | tf_op jit(solution)/shard_map/reduce_scatter | solution.py:86
Sparse Core Ops, SparseCore 0:
  124.4 57.2 reduce-scatter.8
  184.3 60.4 reduce-scatter.10
  247.3 69.5 reduce-scatter.4
  319.8 43.5 reduce-scatter.6
